TPU v7x, 512 devices: a whole 4x4x16 slice. The times are simulated.
512 devices in a mesh: section: 8 (over y_hi, x), seq: 64 (over y_lo, z, core).
Axes of the slice: x: 4, y: 4 (y_hi: 2, y_lo: 2; y = y_hi * 2 + y_lo), z: 16, core: 2. Of those that a mesh axis runs over, the one named last changes fastest.
Arguments:
- cotangent: bfloat16 [8192, 4096], P('seq'), may hold values from -6 to 6
- in_gate: bfloat16 [8, 8192, 4096], P('section', 'seq'), may hold values from -4 to 4
- mid_gate: bfloat16 [8, 8192, 4096], P('section', 'seq'), may hold values from -4 to 4
- layer_inputs: bfloat16 [8, 8192, 4096], P('section', 'seq'), may hold values from -6 to 6
- filters: bfloat16 [8, 128, 256], P('section'), may hold values from -0.5 to 0.5
- steer_second: float32 [8, 4096], P('section', 'seq'), may hold values from 8192 to 131072
- filter_second: float32 [8, 128, 256], P('section', None, 'seq'), may hold values from 32768 to 524288
Outputs:
- steer_step: float32 [8, 4096], P('section', 'seq')
- filter_step: float32 [8, 128, 256], P('section', None, 'seq')
All inputs are finite; a program needn't handle non-finite values.
Results may differ from a plain program's by a relative error of at most 0.0095.
Values may be sent and summed in bfloat16 or wider, within the bound.
A program may use at most 192 MiB of HBM per device.

v0:
```python
import math

import jax
import jax.numpy as jnp
from jax import lax
from jax.sharding import PartitionSpec as P


def from_behind(block, axis, distance):
    devices = range(lax.axis_size(axis))
    route = [(i - distance, i) for i in devices if i - distance in devices]
    return lax.ppermute(block, axis, route)


def band_matrix(kernel, block_len):
    filt_len, group_count = kernel.shape
    span_len = block_len + filt_len
    padded = jnp.concatenate([kernel.T, jnp.zeros((group_count, block_len + 1), kernel.dtype)], 1)
    tiled_rows = jnp.tile(padded, (1, block_len))[:, : block_len * span_len]
    return tiled_rows.reshape(group_count, block_len, span_len)


def to_columns(matrix, group_count):
    row_count, channel_count = matrix.shape
    return matrix.T.reshape(group_count, channel_count // group_count, row_count)


def filter_rows(band_part, extended):
    pieces = [jnp.einsum("gcs,grs->gcr", extended, band_part, preferred_element_type=jnp.float32)]
    if len(pieces) == 1:
        return pieces[0]
    return jnp.concatenate(pieces, 2)


def filter_grad(extended, values, block_len, filt_len):
    group_count = values.shape[0]
    span_len = block_len + filt_len
    pairwise = jnp.einsum("gcr,gcs->grs", values, extended, preferred_element_type=jnp.float32)
    flat_rows = pairwise.reshape(group_count, block_len * span_len)
    flat_rows = jnp.concatenate([flat_rows, jnp.zeros((group_count, block_len), jnp.float32)], 1)
    skewed = flat_rows.reshape(group_count, block_len, span_len + 1)
    total = jnp.sum(skewed[:, :, :filt_len], 1)
    return total.T


def weigh(current, gate_part):
    return (gate_part.astype(jnp.float32) * current.astype(jnp.float32)).astype(jnp.bfloat16)


def finish(current, mid_part, band_part, extended):
    filtered = filter_rows(band_part, extended)
    return (current.astype(jnp.float32) + mid_part.astype(jnp.float32) * filtered).astype(
        jnp.bfloat16
    )


def adagrad(grad_part, second_part):
    return grad_part / jnp.sqrt(second_part + grad_part * grad_part)


def body(cotangent, in_gate, mid_gate, layer_inputs, filters, steer_second, filter_second):
    row_count, channel_count = (in_gate.shape[1], in_gate.shape[2])
    filt_len, group_count = (filters.shape[1], filters.shape[2])
    group_size = channel_count // group_count
    block_len = math.gcd(row_count, 128)
    sections = lax.axis_size("section")
    my_section = lax.axis_index("section")
    last_section = sections - 1
    band_full = band_matrix(filters[0], block_len)
    gate_cols = to_columns(in_gate[0], group_count)
    mid_cols = to_columns(mid_gate[0], group_count)
    input_cols = to_columns(layer_inputs[0], group_count)
    cot_cols = to_columns(cotangent, group_count)
    group_width = group_count // sections

    def one_turn(turn_index, state_now):
        incoming, kept_ext, kept_grad = state_now
        block_index = turn_index - (last_section - my_section)
        inside = jnp.logical_and(block_index >= 0, block_index < sections)
        clipped = jnp.clip(block_index, 0, sections - 1)
        first_group = clipped * group_width
        fresh_block = lax.dynamic_slice_in_dim(cot_cols, first_group, group_width, 0)
        current = jnp.where(my_section == last_section, fresh_block, incoming)
        gate_block = lax.dynamic_slice_in_dim(gate_cols, first_group, group_width, 0)
        mid_block = lax.dynamic_slice_in_dim(mid_cols, first_group, group_width, 0)
        band_block = lax.dynamic_slice_in_dim(band_full, first_group, group_width, 0)
        weighted = weigh(current, gate_block)
        next_rows = from_behind(weighted, "seq", -1)
        extended = jnp.concatenate([weighted, next_rows], 2)
        outgoing = finish(current, mid_block, band_block, extended)
        old_ext = lax.dynamic_slice_in_dim(kept_ext, first_group, group_width, 0)
        old_grad = lax.dynamic_slice_in_dim(kept_grad, first_group, group_width, 0)
        kept_ext = lax.dynamic_update_slice_in_dim(
            kept_ext, jnp.where(inside, extended, old_ext), first_group, 0
        )
        kept_grad = lax.dynamic_update_slice_in_dim(
            kept_grad, jnp.where(inside, outgoing, old_grad), first_group, 0
        )
        passed = from_behind(outgoing, "section", -1)
        return (passed, kept_ext, kept_grad)

    start_state = (
        jnp.zeros((group_width, group_size, row_count), jnp.bfloat16),
        jnp.zeros((group_count, group_size, row_count + filt_len), jnp.bfloat16),
        jnp.zeros((group_count, group_size, row_count), jnp.bfloat16),
    )
    final_state = lax.fori_loop(0, sections + sections - 1, one_turn, start_state)
    values = (mid_cols.astype(jnp.float32) * input_cols.astype(jnp.float32)).astype(jnp.bfloat16)
    local_filter = filter_grad(final_state[1], values, block_len, filt_len)
    local_steer = jnp.sum(final_state[2].astype(jnp.float32), 2).reshape(channel_count)
    steer_part, filter_part = (
        lax.psum_scatter(local_steer, "seq", scatter_dimension=0, tiled=True),
        lax.psum_scatter(local_filter, "seq", scatter_dimension=1, tiled=True),
    )
    return (
        adagrad(steer_part, steer_second[0])[None],
        adagrad(filter_part, filter_second[0])[None],
    )


def solution(mesh):
    in_specs = (
        P("seq", None),
        P("section", "seq", None),
        P("section", "seq", None),
        P("section", "seq", None),
        P("section", None, None),
        P("section", "seq"),
        P("section", None, "seq"),
    )
    out_specs = (P("section", "seq"), P("section", None, "seq"))
    return jax.shard_map(body, mesh=mesh, in_specs=in_specs, out_specs=out_specs, check_vma=False)
```

profile of v0, /device:TPU:1, one launch (start us, length us, event | category | flops | bytes accessed | tf_op | source)
XLA Modules:
  0.0 900.9 jit_solution(507897443627670450)
XLA Ops:
  7.2 2.4 copy.20
  14.9 6.3 tile.4
  21.2 19.2 %tile.10 = bf16[256,32896]{0,1:T(8,128)(2,1)} reshape(bf16[256,128,257]{0,2,1:T(8,128)(2,1)} %tile.4) | data formatting | bytes 33685504 | tf_op jit(solution)/shard_map/tile | solution.py:19
  40.4 13.8 %slice.8 = bf16[256,32768]{0,1:T(8,128)(2,1)} slice(bf16[256,32896]{0,1:T(8,128)(2,1)} %tile.10), slice={[0:256], [0:32768]} | slice | bytes 33554432 | tf_op jit(solution)/shard_map/slice | solution.py:19
  54.3 23.0 %copy.23 = bf16[256,128,256]{2,1,0:T(8,128)(2,1)} copy(bf16[256,128,256]{0,2,1:T(8,128)(2,1)} %bitcast.49) | data formatting | bytes 33554432 | tf_op jit(solution)/shard_map/while | solution.py:107
  78.5 292.0 %while.19 = (s32[]{:T(128)}, bf16[32,16,128]{2,1,0:T(8,128)(2,1)S(1)}, bf16[256,16,256]{2,1,0:T(8,128)(2,1)S(1)}, bf16[256,16,128]{2,1,0:T(8,128)(2,1)}, pred[]{...) while((s32[]{:T(128)}, ...), condition=%wide.region_1.2_spmd, body=%wide.region_0.1_spmd.sunk | while | flops 35520524 | bytes 5507414 | solution.py:107
  79.6 8.7 collective-permute-start
  89.3 3.0 select_dynamic-update-slice_fusion.4
  93.7 5.4 collective-permute-done.1
  100.2 3.1 collective-permute-start
  103.3 3.1 collective-permute-done
  106.5 3.0 select_dynamic-update-slice_fusion.4
  110.9 4.6 collective-permute-done.1
  116.5 1.9 collective-permute-start
  118.4 4.3 collective-permute-done
  122.8 3.0 select_dynamic-update-slice_fusion.4
  127.2 4.5 collective-permute-done.1
  132.7 1.9 collective-permute-start
  134.7 4.4 collective-permute-done
  139.1 3.0 select_dynamic-update-slice_fusion.4
  143.5 4.5 collective-permute-done.1
  151.0 4.3 collective-permute-done
  155.4 3.0 select_dynamic-update-slice_fusion.4
  159.8 7.6 collective-permute-done.1
  168.4 1.9 collective-permute-start
  170.4 4.3 collective-permute-done
  174.7 3.0 select_dynamic-update-slice_fusion.4
  179.1 8.1 collective-permute-done.1
  188.3 1.9 collective-permute-start
  190.2 4.3 collective-permute-done
  194.6 3.0 select_dynamic-update-slice_fusion.4
  199.0 8.1 collective-permute-done.1
  210.1 4.3 collective-permute-done
  214.5 3.0 select_dynamic-update-slice_fusion.4
  218.9 8.1 collective-permute-done.1
  230.0 4.3 collective-permute-done
  234.3 3.0 select_dynamic-update-slice_fusion.4
  238.7 8.2 collective-permute-done.1
  249.8 4.3 collective-permute-done
  254.2 3.0 select_dynamic-update-slice_fusion.4
  258.6 8.2 collective-permute-done.1
  267.8 1.9 collective-permute-start
  269.8 4.3 collective-permute-done
  274.1 3.0 select_dynamic-update-slice_fusion.4
  278.5 8.1 collective-permute-done.1
  289.6 4.8 collective-permute-done
  294.4 3.0 select_dynamic-update-slice_fusion.4
  298.8 8.4 collective-permute-done.1
  310.2 5.3 collective-permute-done
  315.5 3.0 select_dynamic-update-slice_fusion.4
  319.9 8.4 collective-permute-done.1
  331.3 5.3 collective-permute-done
  336.6 3.0 select_dynamic-update-slice_fusion.4
  341.0 8.4 collective-permute-done.1
  352.4 5.3 collective-permute-done
  357.7 3.0 select_dynamic-update-slice_fusion.4
  362.1 8.4 collective-permute-done.1
  370.5 17.2 %fusion.14 = f32[256,128,256]{2,1,0:T(8,128)} fusion(bf16[256,16,256]{2,1,0:T(8,128)(2,1)S(1)} %get-tuple-element.221, f32[256,16,128]{2,1,0:T(8,128)} %bitcast.50, bf16[256,16,128]{2,1,0:T(8,128)(2,1)S(1)} %get-tuple-element.381), kind=kOutput, calls=%fused_computation.17 | convolution fusion | flops 270008320 | bytes 38797312 | tf_op jit(solution)/shard_map/gcr,gcs->grs/dot_general | solution.py:38
  387.7 35.0 %copy.27 = f32[256,128,256]{0,2,1:T(8,128)} copy(f32[256,128,256]{2,1,0:T(8,128)} %fusion.14) | data formatting | bytes 67108864 | tf_op jit(solution)/shard_map/reshape | solution.py:39
  422.7 22.4 %concatenate.16 = f32[256,32896]{0,1:T(8,128)} pad(f32[256,32768]{0,1:T(8,128)} %bitcast.48, f32[]{:T(128)} %constant.72.clone.1), padding=0_0x0_128 | pad | bytes 67239936 | tf_op jit(solution)/shard_map/concatenate | solution.py:40
  445.1 28.3 %reshape.40 = f32[256,128,257]{0,2,1:T(8,128)} reshape(f32[256,32896]{0,1:T(8,128)} %concatenate.16) | data formatting | bytes 67371008 | tf_op jit(solution)/shard_map/reshape | solution.py:41
  473.5 6.9 slice_reduce_fusion
  484.4 218.9 %all-reduce.2 = f32[4096]{0:T(1024)S(1)} all-reduce(f32[4096]{0:T(1024)S(1)} %reshape.38), channel_id=2, replica_groups=mesh['section'=8,'seq'=64] {'seq'}, use_global_device_ids=true, to_apply=%region_3.4.clone | all-reduce | flops 4096 | bytes 32768
  704.0 188.8 %all-reduce.6.cloned.1.call-done = f32[128,256]{0,1:T(8,128)} async-done(((f32[128,256]{0,1:T(8,128)}), f32[128,256]{0,1:T(8,128)}) %all-reduce.6.cloned.1.call-update) | async-done | bytes 131088
  (82 shorter events, 63.5 us)
Async XLA Ops:
  7.2 2.5 copy-start.1
  7.2 885.6 %all-reduce.6.cloned.1.call-start = ((), (), s32[]{:S(2)}) async-start(), calls=%async_computation | async-start | bytes 262144
  7.2 3.7 copy-start.2
  13.1 1.9 copy-start.3
  79.6 9.7 %collective-permute-start = (bf16[32,16,128]{2,1,0:T(8,128)(2,1)S(1)}, bf16[32,16,128]{2,1,0:T(8,128)(2,1)S(1)}, u32[]{:S(2)}, u32[]{:S(2)}) collective-permute-start(bf16[32,16,128]{2,1,0:T(8,128)(2,1)S(1)} %fusion.23), channel_id=1, source_target_pairs={{1,0},{2,1},{3,2},{4,3},{5,4},{6,5},{7,6},{8,7},{9,8},{10,9},{11,1... | collective-permute-start | bytes 393224 | tf_op jit(solution)/shard_map/while/body/eval_jaxpr/ppermute | solution.py:12
  92.4 6.8 collective-permute-start.1
  100.2 6.3 collective-permute-start
  109.5 5.9 collective-permute-start.1
  116.5 6.3 collective-permute-start
  125.8 5.9 collective-permute-start.1
  132.7 6.3 collective-permute-start
  142.1 5.9 collective-permute-start.1
  149.1 6.3 collective-permute-start
  158.4 9.0 collective-permute-start.1
  168.4 6.3 collective-permute-start
  177.8 9.5 %collective-permute-start.1 = (bf16[32,16,128]{2,1,0:T(8,128)(2,1)}, bf16[32,16,128]{2,1,0:T(8,128)(2,1)S(1)}, u32[]{:S(2)}, u32[]{:S(2)}) collective-permute-start(bf16[32,16,128]{2,1,0:T(8,128)(2,1)} %get-tuple-element.327), channel_id=1, source_target_pairs={{64,0},{128,64},{192,128},{256,192},{320,256},{384,320},{448,384},... | collective-permute-start | bytes 393224 | tf_op jit(solution)/shard_map/while/body/eval_jaxpr/ppermute | solution.py:12
  188.3 6.3 collective-permute-start
  197.6 9.5 %collective-permute-start.1 = (bf16[32,16,128]{2,1,0:T(8,128)(2,1)}, bf16[32,16,128]{2,1,0:T(8,128)(2,1)S(1)}, u32[]{:S(2)}, u32[]{:S(2)}) collective-permute-start(bf16[32,16,128]{2,1,0:T(8,128)(2,1)} %get-tuple-element.327), channel_id=1, source_target_pairs={{64,0},{128,64},{192,128},{256,192},{320,256},{384,320},{448,384},... | collective-permute-start | bytes 393224 | tf_op jit(solution)/shard_map/while/body/eval_jaxpr/ppermute | solution.py:12
  208.2 6.3 collective-permute-start
  217.5 9.5 %collective-permute-start.1 = (bf16[32,16,128]{2,1,0:T(8,128)(2,1)}, bf16[32,16,128]{2,1,0:T(8,128)(2,1)S(1)}, u32[]{:S(2)}, u32[]{:S(2)}) collective-permute-start(bf16[32,16,128]{2,1,0:T(8,128)(2,1)} %get-tuple-element.327), channel_id=1, source_target_pairs={{64,0},{128,64},{192,128},{256,192},{320,256},{384,320},{448,384},... | collective-permute-start | bytes 393224 | tf_op jit(solution)/shard_map/while/body/eval_jaxpr/ppermute | solution.py:12
  228.0 6.3 collective-permute-start
  237.3 9.5 %collective-permute-start.1 = (bf16[32,16,128]{2,1,0:T(8,128)(2,1)}, bf16[32,16,128]{2,1,0:T(8,128)(2,1)S(1)}, u32[]{:S(2)}, u32[]{:S(2)}) collective-permute-start(bf16[32,16,128]{2,1,0:T(8,128)(2,1)} %get-tuple-element.327), channel_id=1, source_target_pairs={{64,0},{128,64},{192,128},{256,192},{320,256},{384,320},{448,384},... | collective-permute-start | bytes 393224 | tf_op jit(solution)/shard_map/while/body/eval_jaxpr/ppermute | solution.py:12
  247.9 6.3 collective-permute-start
  257.2 9.6 %collective-permute-start.1 = (bf16[32,16,128]{2,1,0:T(8,128)(2,1)}, bf16[32,16,128]{2,1,0:T(8,128)(2,1)S(1)}, u32[]{:S(2)}, u32[]{:S(2)}) collective-permute-start(bf16[32,16,128]{2,1,0:T(8,128)(2,1)} %get-tuple-element.327), channel_id=1, source_target_pairs={{64,0},{128,64},{192,128},{256,192},{320,256},{384,320},{448,384},... | collective-permute-start | bytes 393224 | tf_op jit(solution)/shard_map/while/body/eval_jaxpr/ppermute | solution.py:12
  267.8 6.3 collective-permute-start
  277.1 9.5 %collective-permute-start.1 = (bf16[32,16,128]{2,1,0:T(8,128)(2,1)}, bf16[32,16,128]{2,1,0:T(8,128)(2,1)S(1)}, u32[]{:S(2)}, u32[]{:S(2)}) collective-permute-start(bf16[32,16,128]{2,1,0:T(8,128)(2,1)} %get-tuple-element.327), channel_id=1, source_target_pairs={{64,0},{128,64},{192,128},{256,192},{320,256},{384,320},{448,384},... | collective-permute-start | bytes 393224 | tf_op jit(solution)/shard_map/while/body/eval_jaxpr/ppermute | solution.py:12
  287.7 6.7 collective-permute-start
  297.4 9.8 %collective-permute-start.1 = (bf16[32,16,128]{2,1,0:T(8,128)(2,1)}, bf16[32,16,128]{2,1,0:T(8,128)(2,1)S(1)}, u32[]{:S(2)}, u32[]{:S(2)}) collective-permute-start(bf16[32,16,128]{2,1,0:T(8,128)(2,1)} %get-tuple-element.327), channel_id=1, source_target_pairs={{64,0},{128,64},{192,128},{256,192},{320,256},{384,320},{448,384},... | collective-permute-start | bytes 393224 | tf_op jit(solution)/shard_map/while/body/eval_jaxpr/ppermute | solution.py:12
  308.3 7.2 collective-permute-start
  318.5 9.8 %collective-permute-start.1 = (bf16[32,16,128]{2,1,0:T(8,128)(2,1)}, bf16[32,16,128]{2,1,0:T(8,128)(2,1)S(1)}, u32[]{:S(2)}, u32[]{:S(2)}) collective-permute-start(bf16[32,16,128]{2,1,0:T(8,128)(2,1)} %get-tuple-element.327), channel_id=1, source_target_pairs={{64,0},{128,64},{192,128},{256,192},{320,256},{384,320},{448,384},... | collective-permute-start | bytes 393224 | tf_op jit(solution)/shard_map/while/body/eval_jaxpr/ppermute | solution.py:12
  329.3 7.2 collective-permute-start
  339.6 9.8 %collective-permute-start.1 = (bf16[32,16,128]{2,1,0:T(8,128)(2,1)}, bf16[32,16,128]{2,1,0:T(8,128)(2,1)S(1)}, u32[]{:S(2)}, u32[]{:S(2)}) collective-permute-start(bf16[32,16,128]{2,1,0:T(8,128)(2,1)} %get-tuple-element.327), channel_id=1, source_target_pairs={{64,0},{128,64},{192,128},{256,192},{320,256},{384,320},{448,384},... | collective-permute-start | bytes 393224 | tf_op jit(solution)/shard_map/while/body/eval_jaxpr/ppermute | solution.py:12
  350.5 7.2 collective-permute-start
  360.7 9.8 %collective-permute-start.1 = (bf16[32,16,128]{2,1,0:T(8,128)(2,1)}, bf16[32,16,128]{2,1,0:T(8,128)(2,1)S(1)}, u32[]{:S(2)}, u32[]{:S(2)}) collective-permute-start(bf16[32,16,128]{2,1,0:T(8,128)(2,1)} %get-tuple-element.327), channel_id=1, source_target_pairs={{64,0},{128,64},{192,128},{256,192},{320,256},{384,320},{448,384},... | collective-permute-start | bytes 393224 | tf_op jit(solution)/shard_map/while/body/eval_jaxpr/ppermute | solution.py:12
  473.5 10.3 %copy-start = (bf16[256,16,128]{2,1,0:T(8,128)(2,1)S(1)}, bf16[256,16,128]{2,1,0:T(8,128)(2,1)}, u32[]{:S(2)}) copy-start(bf16[256,16,128]{2,1,0:T(8,128)(2,1)} %get-tuple-element.220) | copy-start | bytes 3145732
  473.5 229.9 %copy-start.5 = (f32[1,64]{1,0:T(1,128)S(1)}, f32[1,64]{1,0:T(1,128)}, u32[]{:S(2)}) copy-start(f32[1,64]{1,0:T(1,128)} %param.14) | copy-start | bytes 772
  473.5 419.3 %copy-start.4 = (f32[1,128,4]{1,2,0:T(4,128)S(1)}, f32[1,128,4]{1,2,0:T(4,128)}, u32[]{:S(2)}) copy-start(f32[1,128,4]{1,2,0:T(4,128)} %param.15) | copy-start | bytes 6148
Sparse Core Ops, SparseCore 0:
  481.3 411.4 all-reduce.5
where the time goes:
time: 905 us; the launch traced here: 901 us
  waiting for transfers between devices  362 us (40%)
  blocking collectives  219 us (24%)
  local copies, waits for them, and re-layouts  158 us (17%)
  matrix products  62.8 us (7%)
  starting transfers between devices  56.1 us (6%)
  other arithmetic  27.5 us (3%)
  between operations  15.4 us (2%)
    unnamed x1, blocking collectives  219 us
    unnamed x2, waiting for transfers between devices  189 us
    ppermute x30, waiting for transfers between devices, from_behind(): return lax.ppermute(block, axis, route)  173 us
    ppermute x30, starting transfers between devices, from_behind(): return lax.ppermute(block, axis, route)  56 us
    dot_general x15, matrix products, filter_rows(): jnp.einsum('gcs,grs->gcr', extended, band_part, preferred_element_type=jn...  45.6 us
    reshape x1, local copies, waits for them, and re-layouts, filter_grad(): flat_rows = pairwise.reshape(group_count, block_len * span_len)  35 us
    reshape x1, local copies, waits for them, and re-layouts, filter_grad(): skewed = flat_rows.reshape(group_count, block_len, span_len + 1)  28.3 us
    another operation x2, local copies, waits for them, and re-layouts, band_matrix(): tiled_rows = jnp.tile(padded, (1, block_len))[:, :block_len * span_len]  25.5 us
  transfers between devices with their start and end apart: 31, of which 31 were waited for; matrix products, arithmetic and copies ran while one was open for 0% of the time, Pallas kernels for 0%

commit v1 on v0

v1 whole, which is shorter than its diff:
```python
import functools

import jax
import jax.numpy as jnp
from jax import lax
from jax.experimental import pallas as pl
from jax.experimental.pallas import tpu as pltpu
from jax.sharding import PartitionSpec as P

MESH = pl.DeviceIdType.MESH
F32 = jnp.float32
BF16 = jnp.bfloat16
CORES = 2
Y_PARTS = 2
SPLITS = 4
WIDE = 256
GROUP = 16


def iota(shape, dim):
    return lax.broadcasted_iota(jnp.int32, shape, dim)


def kernel(
    sections, seqs,
    cot, in_gate, mid_gate, inputs, filters, out,
    in_all, mid_all, x_all, grad, taps_out, taps_all, toep, ext, rev,
    steer, msg, got, half_in, half_sum, y_in, y_sum, z_in,
    local_sem, a2a_send, a2a_recv, tap_send, tap_recv, halo_send, halo_recv,
    msg_send, msg_recv, core_sem, y_sem, z_send, z_recv,
):
    rows, channels = cot.shape
    mine = channels // sections
    blocks = mine // WIDE
    groups = mine // GROUP
    z_size = seqs // (CORES * Y_PARTS)
    me = lax.axis_index("section")
    q = lax.axis_index("seq")
    core = lax.rem(q, CORES)
    z = lax.rem(lax.div(q, CORES), z_size)
    y = lax.div(q, CORES * z_size)

    def section_peer(step):
        return lax.rem(me + step, sections)

    def z_peer(step):
        return lax.rem(z + step, z_size)

    def seq_at(y_at, z_at, core_at):
        return (y_at * z_size + z_at) * CORES + core_at

    core_peer = seq_at(y, z, 1 - core)
    y_peer = seq_at(1 - y, z, core)
    chip_peer = lax.rem(q + 2 * core - 1 + seqs, seqs)

    sources = (in_gate, mid_gate, inputs)
    targets = (in_all, mid_all, x_all)

    for a in range(3):
        pltpu.make_async_copy(
            sources[a].at[:, pl.ds(pl.multiple_of(me * mine, 128), mine)],
            targets[a].at[me],
            a2a_recv.at[a, me],
        ).start()
    cot_copy = pltpu.make_async_copy(
        cot.at[:, pl.ds(pl.multiple_of(me * mine, 128), mine)], grad, local_sem.at[0]
    )
    cot_copy.start()

    barrier = pltpu.get_barrier_semaphore()
    peers = [(section_peer(d), q) for d in range(1, sections)]
    peers += [(me, core_peer), (me, y_peer), (me, chip_peer)]
    peers += [(me, seq_at(y, z_peer(d), core)) for d in range(1, z_size)]
    for peer in peers:
        pl.semaphore_signal(barrier, inc=1, device_id=peer, device_id_type=MESH)

    taps_t = filters[...].astype(F32).T.astype(BF16)
    for s in range(sections):
        taps_out[s] = taps_t[s * groups : (s + 1) * groups]
    filt_len = taps_out.shape[2]

    @pl.when(q == seqs - 1)
    def _():
        for l in range(sections):
            ext[l, rows : 2 * rows, :] = jnp.zeros((rows, mine), BF16)

    for l in range(sections):
        ext[l, 2 * rows : 3 * rows, :] = jnp.zeros((rows, mine), BF16)
    toep_row = iota((rows, filt_len), 0)
    toep_col = iota((rows, filt_len), 1)
    part = rows // SPLITS
    rev_row, rev_col = iota((rows, rows), 0), iota((rows, rows), 1)
    rev[...] = jnp.where(
        rev_row // part * (2 * part) + part - 1 - rev_row == rev_col, 1.0, 0.0
    ).astype(BF16)

    pl.semaphore_wait(barrier, len(peers))

    def tap_copy(to, layer, step):
        return pltpu.make_async_remote_copy(
            src_ref=taps_out.at[to],
            dst_ref=taps_all.at[layer],
            send_sem=tap_send.at[step],
            recv_sem=tap_recv.at[layer],
            device_id=(to, q),
            device_id_type=MESH,
        )

    def a2a_copy(a, to, layer, step):
        return pltpu.make_async_remote_copy(
            src_ref=sources[a].at[:, pl.ds(pl.multiple_of(to * mine, 128), mine)],
            dst_ref=targets[a].at[layer],
            send_sem=a2a_send.at[a, step],
            recv_sem=a2a_recv.at[a, layer],
            device_id=(to, q),
            device_id_type=MESH,
        )

    pltpu.make_async_copy(taps_out.at[me], taps_all.at[me], tap_recv.at[me]).start()
    for d in range(1, sections):
        tap_copy(section_peer(d), me, d).start()
    for a in range(3):
        for d in range(1, sections):
            a2a_copy(a, section_peer(d), me, d).start()

    def wait_a2a(a, layer):
        a2a_copy(a, section_peer(1), layer, 0).wait_recv()

    def build_toep(layer):
        tap_copy(section_peer(1), layer, 0).wait_recv()
        taps = taps_all[layer].astype(F32)
        near = toep_col >= toep_row
        for g in range(groups):
            wide = jnp.broadcast_to(taps[g : g + 1, :], (rows, filt_len))
            turned = pltpu.roll(wide, 0, 1, stride=1, stride_axis=0)
            b, k = divmod(g, WIDE // GROUP)
            toep[b, k * rows : (k + 1) * rows, 0:rows] = jnp.where(near, turned, 0.0).astype(BF16)
            toep[b, k * rows : (k + 1) * rows, rows : 2 * rows] = jnp.where(
                near, 0.0, turned
            ).astype(BF16)

    def halo_copy(layer, b):
        cols = slice(b * WIDE, (b + 1) * WIDE)
        return pltpu.make_async_remote_copy(
            src_ref=ext.at[layer, 0:rows, cols],
            dst_ref=ext.at[layer, rows : 2 * rows, cols],
            send_sem=halo_send.at[layer, b],
            recv_sem=halo_recv.at[layer, b],
            device_id=(me, lax.rem(q + seqs - 1, seqs)),
            device_id_type=MESH,
        )

    def weigh(layer, b):
        cols = slice(b * WIDE, (b + 1) * WIDE)
        ext[layer, 0:rows, cols] = (
            in_all[layer, :, cols].astype(F32) * grad[:, cols].astype(F32)
        ).astype(BF16)

        @pl.when(q > 0)
        def _():
            halo_copy(layer, b).start()

    lane_group = iota((rows, WIDE), 1) // GROUP

    def advance(layer, b):
        cols = slice(b * WIDE, (b + 1) * WIDE)

        @pl.when(q < seqs - 1)
        def _():
            halo_copy(layer, b).wait_recv()

        window = ext[layer, 0 : 2 * rows, cols]
        filtered = jnp.zeros((rows, WIDE), F32)
        for k in range(WIDE // GROUP):
            full = jnp.dot(
                toep[b, k * rows : (k + 1) * rows, :], window, preferred_element_type=F32
            )
            filtered = jnp.where(lane_group == k, full, filtered)
        fresh = (
            grad[:, cols].astype(F32) + mid_all[layer, :, cols].astype(F32) * filtered
        ).astype(BF16)
        grad[:, cols] = fresh
        steer[0:1, cols] = jnp.sum(fresh.astype(F32), 0, keepdims=True)

    part_col = iota((part, filt_len), 1)
    part_row = part - 1 - iota((part, filt_len), 0)
    part_near = part_col >= part_row
    split_lane = lax.rem(iota((part, SPLITS * 128), 1), 128) // GROUP

    def msg_copy(layer):
        return pltpu.make_async_remote_copy(
            src_ref=msg.at[layer],
            dst_ref=got.at[pl.ds(me * (mine // 128), mine // 128)],
            send_sem=msg_send.at[layer],
            recv_sem=msg_recv.at[me],
            device_id=(layer, q),
            device_id_type=MESH,
        )

    def filter_sums(layer):
        wait_a2a(2, layer)
        values = (mid_all[layer].astype(F32) * x_all[layer].astype(F32)).astype(BF16)
        turned = jnp.dot(rev[...], values, preferred_element_type=F32).astype(BF16)
        for c in range(mine // 128):
            cols = slice(c * 128, (c + 1) * 128)
            left = jnp.concatenate(
                [turned[s * part : (s + 1) * part, cols] for s in range(SPLITS)], 1
            )
            right = jnp.concatenate(
                [ext[layer, s * part : s * part + 2 * rows, cols] for s in range(SPLITS)], 1
            )
            stack = jnp.concatenate(
                [jnp.where(split_lane == k, left, jnp.zeros_like(left)) for k in range(8)], 0
            )
            pairs = lax.dot_general(
                stack, right, (((1,), (1,)), ((), ())), preferred_element_type=F32
            )
            lines = []
            for k in range(8):
                own = pairs[k * part : (k + 1) * part]
                folded = jnp.where(part_near, own[:, :filt_len], own[:, filt_len:])
                moved = pltpu.roll(
                    folded, (filt_len + 1 - part) % filt_len, 1, stride=1, stride_axis=0
                )
                lines.append(jnp.sum(moved, 0, keepdims=True))
            tail = [steer[0:1, cols], jnp.zeros((3, 128), F32)]
            msg[layer, c, 0] = jnp.concatenate(lines[:4] + tail, 0)
            msg[layer, c, 1] = jnp.concatenate(lines[4:] + tail, 0)

        @pl.when(layer != me)
        def _():
            msg_copy(layer).start()

        @pl.when(layer == me)
        def _():
            pltpu.make_async_copy(
                msg.at[layer],
                got.at[pl.ds(me * (mine // 128), mine // 128)],
                msg_recv.at[me],
            ).start()

    last = sections - 1
    cot_copy.wait()
    wait_a2a(0, last)
    for b in range(blocks):
        weigh(last, b)
    build_toep(last)

    def one_layer(turn, carry):
        layer = last - turn
        wait_a2a(1, layer)

        @pl.when(layer > 0)
        def _():
            wait_a2a(0, jnp.maximum(layer - 1, 0))

        for b in range(blocks):
            advance(layer, b)

            @pl.when(layer > 0)
            def _():
                weigh(jnp.maximum(layer - 1, 0), b)

        @pl.when(layer > 0)
        def _():
            build_toep(jnp.maximum(layer - 1, 0))

        filter_sums(layer)
        return carry

    lax.fori_loop(0, sections, one_layer, 0)

    per = mine // 128

    def wait_msg(j):
        pltpu.make_async_remote_copy(
            src_ref=msg.at[0],
            dst_ref=got.at[pl.ds(j * per, per)],
            send_sem=msg_send.at[0],
            recv_sem=msg_recv.at[j],
            device_id=(section_peer(1), q),
            device_id_type=MESH,
        ).wait_recv()

    for j in range(sections):
        wait_msg(j)
    core_copy = pltpu.make_async_remote_copy(
        src_ref=got.at[:, 1 - core],
        dst_ref=half_in,
        send_sem=core_sem.at[0],
        recv_sem=core_sem.at[1],
        device_id=(me, core_peer),
        device_id_type=MESH,
    )
    core_copy.start()
    core_copy.wait()
    half_sum[...] = got[:, core] + half_in[...]
    y_copy = pltpu.make_async_remote_copy(
        src_ref=half_sum.at[pl.ds((1 - y) * z_size, z_size)],
        dst_ref=y_in,
        send_sem=y_sem.at[0],
        recv_sem=y_sem.at[1],
        device_id=(me, y_peer),
        device_id_type=MESH,
    )
    y_copy.start()
    y_copy.wait()
    y_sum[...] = half_sum[pl.ds(y * z_size, z_size)] + y_in[...]

    def z_copy(step):
        to = z_peer(step)
        return pltpu.make_async_remote_copy(
            src_ref=y_sum.at[to],
            dst_ref=z_in.at[z],
            send_sem=z_send.at[step],
            recv_sem=z_recv.at[z],
            device_id=(me, seq_at(y, to, core)),
            device_id_type=MESH,
        )

    for d in range(1, z_size):
        z_copy(d).start()
    total = y_sum[z]
    for d in range(1, z_size):
        origin = z_peer(d)
        pltpu.make_async_remote_copy(
            src_ref=y_sum.at[0],
            dst_ref=z_in.at[origin],
            send_sem=z_send.at[d],
            recv_sem=z_recv.at[origin],
            device_id=(me, core_peer),
            device_id_type=MESH,
        ).wait_recv()
    for d in range(1, z_size):
        total = total + z_in[z_peer(d)]
    out[...] = jnp.where(core == 1, pltpu.roll(total, 64, 1), total)
    out[0:4, :] = total[0:4]

    for d in range(1, sections):
        tap_copy(section_peer(d), me, d).wait_send()
        for a in range(3):
            a2a_copy(a, section_peer(d), me, d).wait_send()
    for d in range(1, z_size):
        z_copy(d).wait_send()

    def drain(layer, carry):
        for b in range(blocks):

            @pl.when(q > 0)
            def _():
                halo_copy(layer, b).wait_send()

        @pl.when(layer != me)
        def _():
            msg_copy(layer).wait_send()

        return carry

    lax.fori_loop(0, sections, drain, 0)


def adagrad(grad_part, second_part):
    return grad_part / jnp.sqrt(second_part + grad_part * grad_part)


def body(sections, seqs, cotangent, in_gate, mid_gate, layer_inputs, filters, steer_second, filter_second):
    rows, channels = cotangent.shape
    filt_len = filters.shape[1]
    mine = channels // sections
    groups = mine // GROUP
    z_size = seqs // (CORES * Y_PARTS)
    assert rows == filt_len == 128 and mine % WIDE == 0
    dma = pltpu.SemaphoreType.DMA
    any_spec = pl.BlockSpec(memory_space=pl.ANY)
    vmem_spec = pl.BlockSpec(memory_space=pltpu.VMEM)
    sums = pl.pallas_call(
        functools.partial(kernel, sections, seqs),
        out_shape=jax.ShapeDtypeStruct((8, 128), F32),
        in_specs=[any_spec] * 4 + [vmem_spec],
        out_specs=vmem_spec,
        scratch_shapes=[
            pltpu.VMEM((sections, rows, mine), BF16),
            pltpu.VMEM((sections, rows, mine), BF16),
            pltpu.VMEM((sections, rows, mine), BF16),
            pltpu.VMEM((rows, mine), BF16),
            pltpu.VMEM((sections, groups, filt_len), BF16),
            pltpu.VMEM((sections, groups, filt_len), BF16),
            pltpu.VMEM((mine // WIDE, WIDE // GROUP * rows, 2 * rows), BF16),
            pltpu.VMEM((sections, 3 * rows, mine), BF16),
            pltpu.VMEM((rows, rows), BF16),
            pltpu.VMEM((8, mine), F32),
            pltpu.VMEM((sections, mine // 128, 2, 8, 128), F32),
            pltpu.VMEM((seqs // 2, 2, 8, 128), F32),
            pltpu.VMEM((seqs // 2, 8, 128), F32),
            pltpu.VMEM((seqs // 2, 8, 128), F32),
            pltpu.VMEM((z_size, 8, 128), F32),
            pltpu.VMEM((z_size, 8, 128), F32),
            pltpu.VMEM((z_size, 8, 128), F32),
            dma((1,)),
            dma((3, sections)),
            dma((3, sections)),
            dma((sections,)),
            dma((sections,)),
            dma((sections, mine // WIDE)),
            dma((sections, mine // WIDE)),
            dma((sections,)),
            dma((sections,)),
            dma((2,)),
            dma((2,)),
            dma((z_size,)),
            dma((z_size,)),
        ],
        compiler_params=pltpu.CompilerParams(
            collective_id=0, has_side_effects=True, vmem_limit_bytes=48 * 2**20
        ),
    )(cotangent, in_gate[0], mid_gate[0], layer_inputs[0], filters[0])
    steer_part = sums[4:5, :64]
    filter_part = sums[0:4].T
    return (
        adagrad(steer_part, steer_second),
        adagrad(filter_part, filter_second[0])[None],
    )


def solution(mesh):
    in_specs = (
        P("seq", None),
        P("section", "seq", None),
        P("section", "seq", None),
        P("section", "seq", None),
        P("section", None, None),
        P("section", "seq"),
        P("section", None, "seq"),
    )
    out_specs = (P("section", "seq"), P("section", None, "seq"))
    step = functools.partial(body, mesh.shape["section"], mesh.shape["seq"])
    return jax.shard_map(step, mesh=mesh, in_specs=in_specs, out_specs=out_specs, check_vma=False)
```

time: 905 us -> 106 us (0.12)
  waiting for transfers between devices: 362 us -> 0 us
  blocking collectives: 219 us -> 0 us
  local copies, waits for them, and re-layouts: 158 us -> 5.74 us
  Pallas kernels: 0 us -> 97.9 us
  matrix products: 62.8 us -> 0 us
  starting transfers between devices: 56.1 us -> 0 us
  other arithmetic: 27.5 us -> 1.11 us
  between operations: 15.4 us -> 0.66 us
    unnamed x1 -> x0, blocking collectives: 219 us -> none
    unnamed x2 -> x0, waiting for transfers between devices: 189 us -> none
    ppermute x30 -> x0, waiting for transfers between devices: 173 us -> none  [from_behind(): return lax.ppermute(block, axis, route)]
    pallas_call x0 -> x1, Pallas kernels: none -> 97.9 us  [body(): pl.pallas_call(functools.partial(kernel, sections, seqs), out_shape=jax.S...]
    reshape x3 -> x0, local copies, waits for them, and re-layouts: 63.4 us -> none  [the longest x1 35 us: filter_grad(): flat_rows = pairwise.reshape(group_count, block_len * span_len)]
    dot_general x16 -> x0, matrix products: 62.8 us -> none  [the longest x15 45.6 us: filter_rows(): jnp.einsum('gcs,grs->gcr', extended, band_part, preferred_element_type=jn...]
    ppermute x30 -> x0, starting transfers between devices: 56 us -> none  [from_behind(): return lax.ppermute(block, axis, route)]
    another operation x2 -> x0, local copies, waits for them, and re-layouts: 25.5 us -> none  [band_matrix(): tiled_rows = jnp.tile(padded, (1, block_len))[:, :block_len * span_len]]
  transfers between devices with their start and end apart: 31 -> 0, of which waited for: 31 -> 0; matrix products, arithmetic and copies ran while one was open for 0% -> 0% of each run, Pallas kernels for 0% -> 0%
where the time goes in v1:
time: 106 us; the launch traced here: 105 us
  Pallas kernels  97.9 us (92%)
  local copies, waits for them, and re-layouts  5.74 us (5%)
  other arithmetic  1.11 us (1%)
    pallas_call x1, Pallas kernels, body(): pl.pallas_call(functools.partial(kernel, sections, seqs), out_shape=jax.S...  97.9 us
    unnamed x14, local copies, waits for them, and re-layouts  5.74 us

profile of v1, /device:TPU:1, one launch (start us, length us, event | category | flops | bytes accessed | tf_op | source)
XLA Modules:
  0.0 105.5 jit_solution(5394948334887341998)
XLA Ops:
  0.6 0.0 copy-start
  0.6 1.2 %copy-done = bf16[128,4096]{1,0:T(8,128)(2,1)S(1)} copy-done((bf16[128,4096]{1,0:T(8,128)(2,1)S(1)}, bf16[128,4096]{1,0:T(8,128)(2,1)}, u32[]{:S(2)}) %copy-start) | copy-done | bytes 1048600
  1.9 0.0 copy-start.1
  1.9 1.2 %copy-done.1 = bf16[1,128,4096]{2,1,0:T(8,128)(2,1)S(1)} copy-done((bf16[1,128,4096]{2,1,0:T(8,128)(2,1)S(1)}, bf16[1,128,4096]{2,1,0:T(8,128)(2,1)}, u32[]{:S(2)}) %copy-start.1) | copy-done | bytes 1048600
  3.1 0.0 copy-start.2
  3.1 1.2 %copy-done.2 = bf16[1,128,4096]{2,1,0:T(8,128)(2,1)S(1)} copy-done((bf16[1,128,4096]{2,1,0:T(8,128)(2,1)S(1)}, bf16[1,128,4096]{2,1,0:T(8,128)(2,1)}, u32[]{:S(2)}) %copy-start.2) | copy-done | bytes 1048600
  4.3 0.0 copy-start.3
  4.3 1.2 %copy-done.3 = bf16[1,128,4096]{2,1,0:T(8,128)(2,1)S(1)} copy-done((bf16[1,128,4096]{2,1,0:T(8,128)(2,1)S(1)}, bf16[1,128,4096]{2,1,0:T(8,128)(2,1)}, u32[]{:S(2)}) %copy-start.3) | copy-done | bytes 1048600
  5.5 0.0 copy-start.4
  5.5 0.8 copy-done.4
  6.4 0.0 copy-start.6
  6.4 0.0 copy-start.5
  6.4 97.9 %shard_map.86 = f32[8,128]{1,0:T(8,128)S(1)} custom-call(bf16[128,4096]{1,0:T(8,128)(2,1)S(1)} %copy-done, bf16[128,4096]{1,0:T(8,128)(2,1)S(1)} %bitcast.19, bf16[128,4096]{1,0:T(8,128)(2,1)S(1)} %bitcast.20, bf16[128,4096]{1,0:T(8,128)(2,1)S(1)} %bitcast.21, bf16[128,256]{1,0:T(8,128)(2,1)S(1)} %bitcast.22), custom_call_target="tpu_custom_call" | custom-call | tf_op jit(solution)/shard_map/pallas_call | solution.py:376
  104.3 0.0 copy-done.6
  104.3 0.5 rsqrt_multiply_fusion
  104.9 0.0 copy-done.5
  104.9 0.6 fusion.2
Async XLA Ops:
  0.6 1.2 %copy-start = (bf16[128,4096]{1,0:T(8,128)(2,1)S(1)}, bf16[128,4096]{1,0:T(8,128)(2,1)}, u32[]{:S(2)}) copy-start(bf16[128,4096]{1,0:T(8,128)(2,1)} %cot.1) | copy-start | bytes 3145732
  1.9 1.2 %copy-start.1 = (bf16[1,128,4096]{2,1,0:T(8,128)(2,1)S(1)}, bf16[1,128,4096]{2,1,0:T(8,128)(2,1)}, u32[]{:S(2)}) copy-start(bf16[1,128,4096]{2,1,0:T(8,128)(2,1)} %param.8) | copy-start | bytes 3145732
  3.1 1.2 %copy-start.2 = (bf16[1,128,4096]{2,1,0:T(8,128)(2,1)S(1)}, bf16[1,128,4096]{2,1,0:T(8,128)(2,1)}, u32[]{:S(2)}) copy-start(bf16[1,128,4096]{2,1,0:T(8,128)(2,1)} %param.9) | copy-start | bytes 3145732
  4.3 1.2 %copy-start.3 = (bf16[1,128,4096]{2,1,0:T(8,128)(2,1)S(1)}, bf16[1,128,4096]{2,1,0:T(8,128)(2,1)}, u32[]{:S(2)}) copy-start(bf16[1,128,4096]{2,1,0:T(8,128)(2,1)} %param.10) | copy-start | bytes 3145732
  5.5 0.8 copy-start.4
  6.4 98.0 %copy-start.6 = (f32[1,64]{1,0:T(1,128)S(1)}, f32[1,64]{1,0:T(1,128)}, u32[]{:S(2)}) copy-start(f32[1,64]{1,0:T(1,128)} %param.12) | copy-start | bytes 772
  6.4 98.5 %copy-start.5 = (f32[1,128,4]{1,2,0:T(4,128)S(1)}, f32[1,128,4]{1,2,0:T(4,128)}, u32[]{:S(2)}) copy-start(f32[1,128,4]{1,2,0:T(4,128)} %param.13) | copy-start | bytes 6148

commit v2 on v1

v2 whole, which is shorter than its diff:
```python
import functools

import jax
import jax.numpy as jnp
from jax import lax
from jax.experimental import pallas as pl
from jax.experimental.pallas import tpu as pltpu
from jax.sharding import PartitionSpec as P

MESH = pl.DeviceIdType.MESH
F32 = jnp.float32
BF16 = jnp.bfloat16
CORES = 2
Y_PARTS = 2
SPLITS = 4
WIDE = 256
GROUP = 16


def iota(shape, dim):
    return lax.broadcasted_iota(jnp.int32, shape, dim)


def kernel(
    sections, seqs,
    cot, in_gate, mid_gate, inputs, filters, out,
    in_all, mid_all, x_all, grad, taps_in, taps_out, taps_all, toep, ext, rev,
    steer, msg, got, near_sum, z_in,
    local_sem, a2a_send, a2a_recv, tap_send, tap_recv, halo_send, halo_recv,
    msg_send, msg_recv, z_send, z_recv,
):
    rows, channels = cot.shape
    mine = channels // sections
    blocks = mine // WIDE
    groups = mine // GROUP
    z_size = seqs // (CORES * Y_PARTS)
    me = lax.axis_index("section")
    q = lax.axis_index("seq")
    core = lax.rem(q, CORES)
    z = lax.rem(lax.div(q, CORES), z_size)
    y = lax.div(q, CORES * z_size)

    def section_peer(step):
        return lax.rem(me + step, sections)

    def z_peer(step):
        return lax.rem(z + step, z_size)

    def seq_at(y_at, z_at, core_at):
        return (y_at * z_size + z_at) * CORES + core_at

    chip_peer = lax.rem(q + 2 * core - 1 + seqs, seqs)

    parcels = []
    for b in range(blocks):
        parcels += [(in_gate, in_all, b * WIDE, WIDE), (mid_gate, mid_all, b * WIDE, WIDE)]
    parcels += [(inputs, x_all, b * WIDE, WIDE) for b in range(blocks)]
    gate_at = {("in", b): 2 * b for b in range(blocks)}
    gate_at.update({("mid", b): 2 * b + 1 for b in range(blocks)})
    gate_at.update({("x", b): 2 * blocks + b for b in range(blocks)})

    def parcel_ends(p, to, layer):
        source, target, first, width = parcels[p]
        start = pl.multiple_of(to * mine + first, 128)
        return source.at[:, pl.ds(start, width)], target.at[layer, :, first : first + width]

    tap_load = pltpu.make_async_copy(filters, taps_in, local_sem.at[1])
    tap_load.start()
    for p in range(len(parcels)):
        source, target = parcel_ends(p, me, me)
        pltpu.make_async_copy(source, target, a2a_recv.at[p, me]).start()
    cot_copy = pltpu.make_async_copy(
        cot.at[:, pl.ds(pl.multiple_of(me * mine, 128), mine)], grad, local_sem.at[0]
    )
    cot_copy.start()

    barrier = pltpu.get_barrier_semaphore()
    peers = [
        (section_peer(d), seq_at(lax.rem(y + dy, Y_PARTS), z, lax.rem(core + dc, CORES)))
        for d in range(sections)
        for dy in range(Y_PARTS)
        for dc in range(CORES)
        if d or dy or dc
    ]
    peers += [(me, chip_peer)]
    peers += [(me, seq_at(y, z_peer(d), core)) for d in range(1, z_size)]
    for peer in peers:
        pl.semaphore_signal(barrier, inc=1, device_id=peer, device_id_type=MESH)

    tap_load.wait()
    taps_t = taps_in[...].astype(F32).T.astype(BF16)
    for s in range(sections):
        taps_out[s] = taps_t[s * groups : (s + 1) * groups]
    filt_len = taps_out.shape[2]

    @pl.when(q == seqs - 1)
    def _():
        for l in range(sections):
            ext[l, rows : 2 * rows, :] = jnp.zeros((rows, mine), BF16)

    for l in range(sections):
        ext[l, 2 * rows : 3 * rows, :] = jnp.zeros((rows, mine), BF16)
    toep_row = iota((rows, filt_len), 0)
    toep_col = iota((rows, filt_len), 1)
    part = rows // SPLITS
    rev_row, rev_col = iota((rows, rows), 0), iota((rows, rows), 1)
    rev[...] = jnp.where(
        rev_row // part * (2 * part) + part - 1 - rev_row == rev_col, 1.0, 0.0
    ).astype(BF16)

    pl.semaphore_wait(barrier, len(peers))

    def tap_copy(to, layer, step):
        return pltpu.make_async_remote_copy(
            src_ref=taps_out.at[to],
            dst_ref=taps_all.at[layer],
            send_sem=tap_send.at[step],
            recv_sem=tap_recv.at[layer],
            device_id=(to, q),
            device_id_type=MESH,
        )

    def a2a_copy(p, to, layer, step):
        source, target = parcel_ends(p, to, layer)
        return pltpu.make_async_remote_copy(
            src_ref=source,
            dst_ref=target,
            send_sem=a2a_send.at[p, step],
            recv_sem=a2a_recv.at[p, layer],
            device_id=(to, q),
            device_id_type=MESH,
        )

    pltpu.make_async_copy(taps_out.at[me], taps_all.at[me], tap_recv.at[me]).start()
    for d in range(1, sections):
        tap_copy(section_peer(d), me, d).start()
    for p in range(len(parcels)):
        for d in range(1, sections):
            a2a_copy(p, section_peer(d), me, d).start()

    def wait_a2a(p, layer):
        a2a_copy(p, section_peer(1), layer, 0).wait_recv()

    def build_toep(layer):
        tap_copy(section_peer(1), layer, 0).wait_recv()
        taps = taps_all[layer].astype(F32)
        near = toep_col >= toep_row
        for g in range(groups):
            wide = jnp.broadcast_to(taps[g : g + 1, :], (rows, filt_len))
            turned = pltpu.roll(wide, 0, 1, stride=1, stride_axis=0)
            b, k = divmod(g, WIDE // GROUP)
            toep[layer, b, k * rows : (k + 1) * rows, 0:rows] = jnp.where(near, turned, 0.0).astype(BF16)
            toep[layer, b, k * rows : (k + 1) * rows, rows : 2 * rows] = jnp.where(
                near, 0.0, turned
            ).astype(BF16)

    def halo_copy(layer, b):
        cols = slice(b * WIDE, (b + 1) * WIDE)
        return pltpu.make_async_remote_copy(
            src_ref=ext.at[layer, 0:rows, cols],
            dst_ref=ext.at[layer, rows : 2 * rows, cols],
            send_sem=halo_send.at[layer, b],
            recv_sem=halo_recv.at[layer, b],
            device_id=(me, lax.rem(q + seqs - 1, seqs)),
            device_id_type=MESH,
        )

    def weigh(layer, b):
        cols = slice(b * WIDE, (b + 1) * WIDE)
        wait_a2a(gate_at["in", b], layer)
        ext[layer, 0:rows, cols] = (
            in_all[layer, :, cols].astype(F32) * grad[:, cols].astype(F32)
        ).astype(BF16)

        @pl.when(q > 0)
        def _():
            halo_copy(layer, b).start()

    lane_group = iota((rows, WIDE), 1) // GROUP

    def advance(layer, b):
        cols = slice(b * WIDE, (b + 1) * WIDE)

        @pl.when(q < seqs - 1)
        def _():
            halo_copy(layer, b).wait_recv()

        window = ext[layer, 0 : 2 * rows, cols]
        filtered = jnp.zeros((rows, WIDE), F32)
        for k in range(WIDE // GROUP):
            full = jnp.dot(
                toep[layer, b, k * rows : (k + 1) * rows, :], window, preferred_element_type=F32
            )
            filtered = jnp.where(lane_group == k, full, filtered)
        wait_a2a(gate_at["mid", b], layer)
        fresh = (
            grad[:, cols].astype(F32) + mid_all[layer, :, cols].astype(F32) * filtered
        ).astype(BF16)
        grad[:, cols] = fresh
        steer[layer, :, cols] = jnp.sum(fresh.astype(F32), 0, keepdims=True)

    part_col = iota((part, filt_len), 1)
    part_row = part - 1 - iota((part, filt_len), 0)
    part_near = part_col >= part_row
    split_lane = lax.rem(iota((part, SPLITS * 128), 1), 128) // GROUP

    y_home = lax.div(me * Y_PARTS, sections)
    lane = lax.rem(me, sections // Y_PARTS)

    def msg_copy(layer, half):
        return pltpu.make_async_remote_copy(
            src_ref=msg.at[layer, half],
            dst_ref=got.at[lane, y, core],
            send_sem=msg_send.at[layer, half],
            recv_sem=msg_recv.at[lane, y, core],
            device_id=(layer, seq_at(y_home, z, half)),
            device_id_type=MESH,
        )

    def stays(layer, half):
        return jnp.logical_and(layer == me, jnp.logical_and(y_home == y, core == half))

    def filter_sums(layer, b):
        wide_cols = slice(b * WIDE, (b + 1) * WIDE)
        wait_a2a(gate_at["x", b], layer)
        values = (
            mid_all[layer, :, wide_cols].astype(F32) * x_all[layer, :, wide_cols].astype(F32)
        ).astype(BF16)
        turned = jnp.dot(rev[...], values, preferred_element_type=F32).astype(BF16)
        for inner in range(WIDE // 128):
            c = b * (WIDE // 128) + inner
            cols = slice(c * 128, (c + 1) * 128)
            own_cols = slice(inner * 128, (inner + 1) * 128)
            left = jnp.concatenate(
                [turned[s * part : (s + 1) * part, own_cols] for s in range(SPLITS)], 1
            )
            right = jnp.concatenate(
                [ext[layer, s * part : s * part + 2 * rows, cols] for s in range(SPLITS)], 1
            )
            stack = jnp.concatenate(
                [jnp.where(split_lane == k, left, jnp.zeros_like(left)) for k in range(8)], 0
            )
            pairs = lax.dot_general(
                stack, right, (((1,), (1,)), ((), ())), preferred_element_type=F32
            )
            lines = []
            for k in range(8):
                own = pairs[k * part : (k + 1) * part]
                folded = jnp.where(part_near, own[:, :filt_len], own[:, filt_len:])
                moved = pltpu.roll(
                    folded, (filt_len + 1 - part) % filt_len, 1, stride=1, stride_axis=0
                )
                lines.append(jnp.sum(moved, 0, keepdims=True))
            tail = [steer[layer, :, cols], jnp.zeros((3, 128), F32)]
            msg[layer, 0, c] = jnp.concatenate(lines[:4] + tail, 0)
            msg[layer, 1, c] = jnp.concatenate(lines[4:] + tail, 0)

    def send_sums(layer):
        for half in range(CORES):
            here = stays(layer, half)

            @pl.when(jnp.logical_not(here))
            def _():
                msg_copy(layer, half).start()

            @pl.when(here)
            def _():
                pltpu.make_async_copy(
                    msg.at[layer, half], got.at[lane, y, core], msg_recv.at[lane, y, core]
                ).start()

    last = sections - 1
    cot_copy.wait()

    def build_one(turn, carry):
        build_toep(last - turn)
        return carry

    lax.fori_loop(0, sections, build_one, 0)
    weigh(last, 0)

    def move(layer, b):
        advance(layer, b)

        @pl.when(layer > 0)
        def _():
            weigh(jnp.maximum(layer - 1, 0), b)

    def lead(turn, carry):
        move(last - turn, 0)
        return carry

    def sums_of(b):
        def sums(step, inner):
            filter_sums(last - step, b)
            if b == blocks - 1:
                send_sums(last - step)
            return inner

        return sums

    def trail(turn, carry):
        first, stop = 2 * (turn - 3), 2 * (turn - 2)
        lax.fori_loop(
            jnp.clip(first, 0, sections), jnp.clip(stop, 0, sections), sums_of(0), 0
        )
        lax.fori_loop(
            jnp.maximum(2 * (turn - last + 1), 0),
            jnp.clip(2 + (last - 2) * (turn - last + 1), 0, last),
            sums_of(1),
            0,
        )
        move(last - turn, 1)
        return carry

    lax.fori_loop(0, sections, lead, 0)
    weigh(last, 1)
    lax.fori_loop(0, sections, trail, 0)
    filter_sums(0, 1)
    send_sums(0)

    lanes = sections // Y_PARTS
    for j in range(lanes):
        chunk = jnp.zeros(got.shape[3:], F32)
        for dy in range(Y_PARTS):
            for dc in range(CORES):
                pltpu.make_async_remote_copy(
                    src_ref=msg.at[0, 0],
                    dst_ref=got.at[j, dy, dc],
                    send_sem=msg_send.at[0, 0],
                    recv_sem=msg_recv.at[j, dy, dc],
                    device_id=(section_peer(1), q),
                    device_id_type=MESH,
                ).wait_recv()
                chunk = chunk + got[j, dy, dc]
        near_sum[j * (mine // 128) : (j + 1) * (mine // 128)] = chunk

    def z_copy(step):
        to = z_peer(step)
        return pltpu.make_async_remote_copy(
            src_ref=near_sum.at[to],
            dst_ref=z_in.at[z],
            send_sem=z_send.at[step],
            recv_sem=z_recv.at[z],
            device_id=(me, seq_at(y, to, core)),
            device_id_type=MESH,
        )

    for d in range(1, z_size):
        z_copy(d).start()
    total = near_sum[z]
    for d in range(1, z_size):
        origin = z_peer(d)
        pltpu.make_async_remote_copy(
            src_ref=near_sum.at[0],
            dst_ref=z_in.at[origin],
            send_sem=z_send.at[d],
            recv_sem=z_recv.at[origin],
            device_id=(me, chip_peer),
            device_id_type=MESH,
        ).wait_recv()
    for d in range(1, z_size):
        total = total + z_in[z_peer(d)]
    out[...] = jnp.where(core == 1, pltpu.roll(total, 64, 1), total)
    out[0:4, :] = total[0:4]

    for d in range(1, sections):
        tap_copy(section_peer(d), me, d).wait_send()
        for p in range(len(parcels)):
            a2a_copy(p, section_peer(d), me, d).wait_send()
    for d in range(1, z_size):
        z_copy(d).wait_send()

    def drain(layer, carry):
        for b in range(blocks):

            @pl.when(q > 0)
            def _():
                halo_copy(layer, b).wait_send()

        for half in range(CORES):

            @pl.when(jnp.logical_not(stays(layer, half)))
            def _():
                msg_copy(layer, half).wait_send()

        return carry

    lax.fori_loop(0, sections, drain, 0)


def adagrad(grad_part, second_part):
    return grad_part / jnp.sqrt(second_part + grad_part * grad_part)


def body(sections, seqs, cotangent, in_gate, mid_gate, layer_inputs, filters, steer_second, filter_second):
    rows, channels = cotangent.shape
    filt_len = filters.shape[1]
    mine = channels // sections
    groups = mine // GROUP
    z_size = seqs // (CORES * Y_PARTS)
    assert rows == filt_len == 128 and mine == 2 * WIDE
    dma = pltpu.SemaphoreType.DMA
    hbm_spec = pl.BlockSpec(memory_space=pltpu.HBM)
    vmem_spec = pl.BlockSpec(memory_space=pltpu.VMEM)
    sums = pl.pallas_call(
        functools.partial(kernel, sections, seqs),
        out_shape=jax.ShapeDtypeStruct((8, 128), F32),
        in_specs=[hbm_spec] * 5,
        out_specs=vmem_spec,
        scratch_shapes=[
            pltpu.VMEM((sections, rows, mine), BF16),
            pltpu.VMEM((sections, rows, mine), BF16),
            pltpu.VMEM((sections, rows, mine), BF16),
            pltpu.VMEM((rows, mine), BF16),
            pltpu.VMEM((filt_len, channels // GROUP), BF16),
            pltpu.VMEM((sections, groups, filt_len), BF16),
            pltpu.VMEM((sections, groups, filt_len), BF16),
            pltpu.VMEM((sections, mine // WIDE, WIDE // GROUP * rows, 2 * rows), BF16),
            pltpu.VMEM((sections, 3 * rows, mine), BF16),
            pltpu.VMEM((rows, rows), BF16),
            pltpu.VMEM((sections, 1, mine), F32),
            pltpu.VMEM((sections, CORES, mine // 128, 8, 128), F32),
            pltpu.VMEM((sections // Y_PARTS, Y_PARTS, CORES, mine // 128, 8, 128), F32),
            pltpu.VMEM((z_size, 8, 128), F32),
            pltpu.VMEM((z_size, 8, 128), F32),
            dma((2,)),
            dma((3 * mine // WIDE, sections)),
            dma((3 * mine // WIDE, sections)),
            dma((sections,)),
            dma((sections,)),
            dma((sections, mine // WIDE)),
            dma((sections, mine // WIDE)),
            dma((sections, CORES)),
            dma((sections // Y_PARTS, Y_PARTS, CORES)),
            dma((z_size,)),
            dma((z_size,)),
        ],
        compiler_params=pltpu.CompilerParams(
            collective_id=0, has_side_effects=True, vmem_limit_bytes=63 * 2**20
        ),
    )(cotangent, in_gate[0], mid_gate[0], layer_inputs[0], filters[0])
    steer_part = sums[4:5, :64]
    filter_part = sums[0:4].T
    return (
        adagrad(steer_part, steer_second),
        adagrad(filter_part, filter_second[0])[None],
    )


def solution(mesh):
    in_specs = (
        P("seq", None),
        P("section", "seq", None),
        P("section", "seq", None),
        P("section", "seq", None),
        P("section", None, None),
        P("section", "seq"),
        P("section", None, "seq"),
    )
    out_specs = (P("section", "seq"), P("section", None, "seq"))
    step = functools.partial(body, mesh.shape["section"], mesh.shape["seq"])
    return jax.shard_map(step, mesh=mesh, in_specs=in_specs, out_specs=out_specs, check_vma=False)
```

time: 106 us -> 114 us (1.075)
  Pallas kernels: 97.9 us -> 111 us
  local copies, waits for them, and re-layouts: 5.74 us -> 0.01 us
  other arithmetic: 1.11 us -> 2.45 us
    pallas_call x1, Pallas kernels: 97.9 us -> 111 us  [body(): pl.pallas_call(functools.partial(kernel, sections, seqs), out_shape=jax.S...]
    unnamed x14 -> x4, local copies, waits for them, and re-layouts: 5.74 us -> 0.01 us
where the time goes in v2:
time: 114 us
  Pallas kernels  111 us (97%)
  other arithmetic  2.45 us (2%)
    pallas_call x1, Pallas kernels, body(): pl.pallas_call(functools.partial(kernel, sections, seqs), out_shape=jax.S...  111 us

profile of v2, /device:TPU:1, one launch (start us, length us, event | category | flops | bytes accessed | tf_op | source)
XLA Modules:
  0.0 114.0 jit_solution(3505015380868350359)
XLA Ops:
  0.6 0.0 copy-start.1
  0.6 0.0 copy-start
  0.7 110.8 %shard_map.86 = f32[8,128]{1,0:T(8,128)} custom-call(bf16[128,4096]{1,0:T(8,128)(2,1)} %cot.1, bf16[128,4096]{1,0:T(8,128)(2,1)} %bitcast.19, bf16[128,4096]{1,0:T(8,128)(2,1)} %bitcast.20, bf16[128,4096]{1,0:T(8,128)(2,1)} %bitcast.21, bf16[128,256]{1,0:T(8,128)(2,1)} %bitcast.22), custom_call_target="tpu_custom_call" | custom-call | tf_op jit(solution)/shard_map/pallas_call | solution.py:406
  111.5 0.0 copy-done.1
  111.5 1.2 %rsqrt_multiply_fusion = f32[1,64]{1,0:T(1,128)} fusion(f32[1,64]{1,0:T(1,128)S(1)} %copy-done.1, f32[8,128]{1,0:T(8,128)} %shard_map.86), kind=kLoop, calls=%fused_computation.5 | loop fusion | flops 192 | bytes 768 | tf_op jit(solution)/shard_map/div | solution.py:393
  112.7 0.0 copy-done
  112.7 1.3 %fusion.2 = f32[1,128,4]{1,2,0:T(4,128)} fusion(f32[1,128,4]{1,2,0:T(4,128)S(1)} %copy-done, f32[8,128]{1,0:T(8,128)} %shard_map.86), kind=kLoop, calls=%fused_computation.3 | loop fusion | flops 1536 | bytes 6144 | tf_op jit(solution)/shard_map/broadcast_in_dim | solution.py:447
Async XLA Ops:
  0.6 110.9 %copy-start.1 = (f32[1,64]{1,0:T(1,128)S(1)}, f32[1,64]{1,0:T(1,128)}, u32[]{:S(2)}) copy-start(f32[1,64]{1,0:T(1,128)} %param.12) | copy-start | bytes 772
  0.6 112.1 %copy-start = (f32[1,128,4]{1,2,0:T(4,128)S(1)}, f32[1,128,4]{1,2,0:T(4,128)}, u32[]{:S(2)}) copy-start(f32[1,128,4]{1,2,0:T(4,128)} %param.13) | copy-start | bytes 6148

commit v3 on v2

--- a/solution.py
+++ b/solution.py
@@ -24,9 +24,9 @@
 def kernel(
     sections, seqs,
     cot, in_gate, mid_gate, inputs, filters, out,
-    in_all, mid_all, x_all, grad, taps_in, taps_out, taps_all, toep, ext, rev,
+    in_stage, mid_stage, x_stage, in_all, mid_all, x_all, grad, taps_in, taps_out, taps_all, toep, ext, rev,
     steer, msg, got, near_sum, z_in,
-    local_sem, a2a_send, a2a_recv, tap_send, tap_recv, halo_send, halo_recv,
+    local_sem, stage_sem, a2a_send, a2a_recv, tap_send, tap_recv, halo_send, halo_recv,
     msg_send, msg_recv, z_send, z_recv,
 ):
     rows, channels = cot.shape
@@ -40,8 +40,11 @@
     z = lax.rem(lax.div(q, CORES), z_size)
     y = lax.div(q, CORES * z_size)
 
+    row = sections // 2
+
     def section_peer(step):
-        return lax.rem(me + step, sections)
+        half = lax.rem(lax.div(me, row) + step // row, 2)
+        return half * row + lax.rem(lax.rem(me, row) + step % row, row)
 
     def z_peer(step):
         return lax.rem(z + step, z_size)
@@ -51,24 +54,36 @@
 
     chip_peer = lax.rem(q + 2 * core - 1 + seqs, seqs)
 
-    parcels = []
-    for b in range(blocks):
-        parcels += [(in_gate, in_all, b * WIDE, WIDE), (mid_gate, mid_all, b * WIDE, WIDE)]
-    parcels += [(inputs, x_all, b * WIDE, WIDE) for b in range(blocks)]
-    gate_at = {("in", b): 2 * b for b in range(blocks)}
-    gate_at.update({("mid", b): 2 * b + 1 for b in range(blocks)})
-    gate_at.update({("x", b): 2 * blocks + b for b in range(blocks)})
+    parcels = [(0, in_all, 0, mine), (1, mid_all, 0, mine), (2, x_all, 0, mine)]
+
+    sources = (in_stage, mid_stage, x_stage)
+    stage_loads = [
+        [
+            pltpu.make_async_copy(
+                whole.at[pl.ds(part * 32, 32)], stage.at[pl.ds(part * 32, 32)], stage_sem.at[a]
+            )
+            for part in range(rows // 32)
+        ]
+        for a, (whole, stage) in enumerate(zip((in_gate, mid_gate, inputs), sources))
+    ]
 
     def parcel_ends(p, to, layer):
         source, target, first, width = parcels[p]
         start = pl.multiple_of(to * mine + first, 128)
-        return source.at[:, pl.ds(start, width)], target.at[layer, :, first : first + width]
+        return sources[source].at[:, pl.ds(start, width)], target.at[layer, :, first : first + width]
 
     tap_load = pltpu.make_async_copy(filters, taps_in, local_sem.at[1])
     tap_load.start()
-    for p in range(len(parcels)):
-        source, target = parcel_ends(p, me, me)
-        pltpu.make_async_copy(source, target, a2a_recv.at[p, me]).start()
+    for a in range(3):
+        for load in stage_loads[a]:
+            load.start()
+    for p, (a, all_layers, first, width) in enumerate(parcels):
+        start = pl.multiple_of(me * mine + first, 128)
+        pltpu.make_async_copy(
+            (in_gate, mid_gate, inputs)[a].at[:, pl.ds(start, width)],
+            all_layers.at[me, :, first : first + width],
+            a2a_recv.at[p, me],
+        ).start()
     cot_copy = pltpu.make_async_copy(
         cot.at[:, pl.ds(pl.multiple_of(me * mine, 128), mine)], grad, local_sem.at[0]
     )
@@ -134,8 +149,11 @@
     pltpu.make_async_copy(taps_out.at[me], taps_all.at[me], tap_recv.at[me]).start()
     for d in range(1, sections):
         tap_copy(section_peer(d), me, d).start()
-    for p in range(len(parcels)):
-        for d in range(1, sections):
+    for a in range(3):
+        for load in stage_loads[a]:
+            load.wait()
+    for p in range(2):
+        for d in (*range(row, sections), *range(1, row)):
             a2a_copy(p, section_peer(d), me, d).start()
 
     def wait_a2a(p, layer):
@@ -167,7 +185,8 @@
 
     def weigh(layer, b):
         cols = slice(b * WIDE, (b + 1) * WIDE)
-        wait_a2a(gate_at["in", b], layer)
+        if b == 0:
+            wait_a2a(0, layer)
         ext[layer, 0:rows, cols] = (
             in_all[layer, :, cols].astype(F32) * grad[:, cols].astype(F32)
         ).astype(BF16)
@@ -192,7 +211,8 @@
                 toep[layer, b, k * rows : (k + 1) * rows, :], window, preferred_element_type=F32
             )
             filtered = jnp.where(lane_group == k, full, filtered)
-        wait_a2a(gate_at["mid", b], layer)
+        if b == 0:
+            wait_a2a(1, layer)
         fresh = (
             grad[:, cols].astype(F32) + mid_all[layer, :, cols].astype(F32) * filtered
         ).astype(BF16)
@@ -220,19 +240,14 @@
     def stays(layer, half):
         return jnp.logical_and(layer == me, jnp.logical_and(y_home == y, core == half))
 
-    def filter_sums(layer, b):
-        wide_cols = slice(b * WIDE, (b + 1) * WIDE)
-        wait_a2a(gate_at["x", b], layer)
-        values = (
-            mid_all[layer, :, wide_cols].astype(F32) * x_all[layer, :, wide_cols].astype(F32)
-        ).astype(BF16)
+    def filter_sums(layer):
+        wait_a2a(2, layer)
+        values = (mid_all[layer].astype(F32) * x_all[layer].astype(F32)).astype(BF16)
         turned = jnp.dot(rev[...], values, preferred_element_type=F32).astype(BF16)
-        for inner in range(WIDE // 128):
-            c = b * (WIDE // 128) + inner
+        for c in range(mine // 128):
             cols = slice(c * 128, (c + 1) * 128)
-            own_cols = slice(inner * 128, (inner + 1) * 128)
             left = jnp.concatenate(
-                [turned[s * part : (s + 1) * part, own_cols] for s in range(SPLITS)], 1
+                [turned[s * part : (s + 1) * part, cols] for s in range(SPLITS)], 1
             )
             right = jnp.concatenate(
                 [ext[layer, s * part : s * part + 2 * rows, cols] for s in range(SPLITS)], 1
@@ -255,7 +270,6 @@
             msg[layer, 0, c] = jnp.concatenate(lines[:4] + tail, 0)
             msg[layer, 1, c] = jnp.concatenate(lines[4:] + tail, 0)
 
-    def send_sums(layer):
         for half in range(CORES):
             here = stays(layer, half)
 
@@ -277,47 +291,38 @@
         return carry
 
     lax.fori_loop(0, sections, build_one, 0)
-    weigh(last, 0)
-
-    def move(layer, b):
-        advance(layer, b)
-
-        @pl.when(layer > 0)
+    for b in range(blocks):
+        weigh(last, b)
+
+    def sums(step, carry):
+        filter_sums(last - step)
+        return carry
+
+    def one_layer(turn, carry):
+        @pl.when(turn == 0)
         def _():
-            weigh(jnp.maximum(layer - 1, 0), b)
-
-    def lead(turn, carry):
-        move(last - turn, 0)
+            for d in range(row, sections):
+                a2a_copy(2, section_peer(d), me, d).start()
+
+        @pl.when(jnp.logical_and(turn > 0, turn < row))
+        def _():
+            step = jnp.clip(turn, 1, row - 1)
+            a2a_copy(2, section_peer(step), me, step).start()
+
+        late = 2 * (turn - 5)
+        lax.fori_loop(jnp.maximum(late, 0), jnp.maximum(late + 2, 0), sums, 0)
+        layer = last - turn
+        for b in range(blocks):
+            advance(layer, b)
+
+            @pl.when(layer > 0)
+            def _():
+                weigh(jnp.maximum(layer - 1, 0), b)
+
         return carry
 
-    def sums_of(b):
-        def sums(step, inner):
-            filter_sums(last - step, b)
-            if b == blocks - 1:
-                send_sums(last - step)
-            return inner
-
-        return sums
-
-    def trail(turn, carry):
-        first, stop = 2 * (turn - 3), 2 * (turn - 2)
-        lax.fori_loop(
-            jnp.clip(first, 0, sections), jnp.clip(stop, 0, sections), sums_of(0), 0
-        )
-        lax.fori_loop(
-            jnp.maximum(2 * (turn - last + 1), 0),
-            jnp.clip(2 + (last - 2) * (turn - last + 1), 0, last),
-            sums_of(1),
-            0,
-        )
-        move(last - turn, 1)
-        return carry
-
-    lax.fori_loop(0, sections, lead, 0)
-    weigh(last, 1)
-    lax.fori_loop(0, sections, trail, 0)
-    filter_sums(0, 1)
-    send_sums(0)
+    lax.fori_loop(0, sections, one_layer, 0)
+    lax.fori_loop(sections - 2, sections, sums, 0)
 
     lanes = sections // Y_PARTS
     for j in range(lanes):
@@ -409,6 +414,9 @@
         in_specs=[hbm_spec] * 5,
         out_specs=vmem_spec,
         scratch_shapes=[
+            pltpu.VMEM((rows, channels), BF16),
+            pltpu.VMEM((rows, channels), BF16),
+            pltpu.VMEM((rows, channels), BF16),
             pltpu.VMEM((sections, rows, mine), BF16),
             pltpu.VMEM((sections, rows, mine), BF16),
             pltpu.VMEM((sections, rows, mine), BF16),
@@ -425,8 +433,9 @@
             pltpu.VMEM((z_size, 8, 128), F32),
             pltpu.VMEM((z_size, 8, 128), F32),
             dma((2,)),
-            dma((3 * mine // WIDE, sections)),
-            dma((3 * mine // WIDE, sections)),
+            dma((3,)),
+            dma((3, sections)),
+            dma((3, sections)),
             dma((sections,)),
             dma((sections,)),
             dma((sections, mine // WIDE)),

time: 114 us -> 96.1 us (0.84)
  Pallas kernels: 111 us -> 92.7 us
    pallas_call x1, Pallas kernels: 111 us -> 92.7 us  [body(): pl.pallas_call(functools.partial(kernel, sections, seqs), out_shape=jax.S...]
where the time goes in v3:
time: 96.1 us; the launch traced here: 95.8 us
  Pallas kernels  92.7 us (96%)
  other arithmetic  2.45 us (3%)
    pallas_call x1, Pallas kernels, body(): pl.pallas_call(functools.partial(kernel, sections, seqs), out_shape=jax.S...  92.7 us

profile of v3, /device:TPU:1, one launch (start us, length us, event | category | flops | bytes accessed | tf_op | source)
XLA Modules:
  0.0 95.8 jit_solution(6066905953432090260)
XLA Ops:
  0.6 0.0 copy-start.1
  0.6 0.0 copy-start
  0.7 92.7 %shard_map.86 = f32[8,128]{1,0:T(8,128)} custom-call(bf16[128,4096]{1,0:T(8,128)(2,1)} %cot.1, bf16[128,4096]{1,0:T(8,128)(2,1)} %bitcast.19, bf16[128,4096]{1,0:T(8,128)(2,1)} %bitcast.20, bf16[128,4096]{1,0:T(8,128)(2,1)} %bitcast.21, bf16[128,256]{1,0:T(8,128)(2,1)} %bitcast.22), custom_call_target="tpu_custom_call" | custom-call | tf_op jit(solution)/shard_map/pallas_call | solution.py:411
  93.4 0.0 copy-done.1
  93.4 1.2 %rsqrt_multiply_fusion = f32[1,64]{1,0:T(1,128)} fusion(f32[1,64]{1,0:T(1,128)S(1)} %copy-done.1, f32[8,128]{1,0:T(8,128)} %shard_map.86), kind=kLoop, calls=%fused_computation.5 | loop fusion | flops 192 | bytes 768 | tf_op jit(solution)/shard_map/div | solution.py:398
  94.6 0.0 copy-done
  94.6 1.3 %fusion.2 = f32[1,128,4]{1,2,0:T(4,128)} fusion(f32[1,128,4]{1,2,0:T(4,128)S(1)} %copy-done, f32[8,128]{1,0:T(8,128)} %shard_map.86), kind=kLoop, calls=%fused_computation.3 | loop fusion | flops 1536 | bytes 6144 | tf_op jit(solution)/shard_map/broadcast_in_dim | solution.py:456
Async XLA Ops:
  0.6 92.7 %copy-start.1 = (f32[1,64]{1,0:T(1,128)S(1)}, f32[1,64]{1,0:T(1,128)}, u32[]{:S(2)}) copy-start(f32[1,64]{1,0:T(1,128)} %param.12) | copy-start | bytes 772
  0.6 93.9 %copy-start = (f32[1,128,4]{1,2,0:T(4,128)S(1)}, f32[1,128,4]{1,2,0:T(4,128)}, u32[]{:S(2)}) copy-start(f32[1,128,4]{1,2,0:T(4,128)} %param.13) | copy-start | bytes 6148

commit v4 on v3

--- a/solution.py
+++ b/solution.py
@@ -156,6 +156,11 @@
         for d in (*range(row, sections), *range(1, row)):
             a2a_copy(p, section_peer(d), me, d).start()
 
+    @pl.when(me >= row)
+    def _():
+        for d in range(row, sections):
+            a2a_copy(2, section_peer(d), me, d).start()
+
     def wait_a2a(p, layer):
         a2a_copy(p, section_peer(1), layer, 0).wait_recv()
 
@@ -299,7 +304,7 @@
         return carry
 
     def one_layer(turn, carry):
-        @pl.when(turn == 0)
+        @pl.when(jnp.logical_and(turn == 0, me < row))
         def _():
             for d in range(row, sections):
                 a2a_copy(2, section_peer(d), me, d).start()
@@ -309,8 +314,8 @@
             step = jnp.clip(turn, 1, row - 1)
             a2a_copy(2, section_peer(step), me, step).start()
 
-        late = 2 * (turn - 5)
-        lax.fori_loop(jnp.maximum(late, 0), jnp.maximum(late + 2, 0), sums, 0)
+        late = 2 * (turn - 4)
+        lax.fori_loop(jnp.maximum(late, 0), jnp.clip(late + 2, 0, last), sums, 0)
         layer = last - turn
         for b in range(blocks):
             advance(layer, b)
@@ -322,7 +327,7 @@
         return carry
 
     lax.fori_loop(0, sections, one_layer, 0)
-    lax.fori_loop(sections - 2, sections, sums, 0)
+    filter_sums(0)
 
     lanes = sections // Y_PARTS
     for j in range(lanes):

time: 96.1 us -> 93.6 us (0.974)
  Pallas kernels: 92.7 us -> 90.2 us
    pallas_call x1, Pallas kernels: 92.7 us -> 90.2 us  [body(): pl.pallas_call(functools.partial(kernel, sections, seqs), out_shape=jax.S...]
where the time goes in v4:
time: 93.6 us; the launch traced here: 93.4 us
  Pallas kernels  90.2 us (96%)
  other arithmetic  2.45 us (3%)
    pallas_call x1, Pallas kernels, body(): pl.pallas_call(functools.partial(kernel, sections, seqs), out_shape=jax.S...  90.2 us

profile of v4, /device:TPU:1, one launch (start us, length us, event | category | flops | bytes accessed | tf_op | source)
XLA Modules:
  0.0 93.4 jit_solution(9306021039893669733)
XLA Ops:
  0.6 0.0 copy-start.1
  0.6 0.0 copy-start
  0.7 90.2 %shard_map.86 = f32[8,128]{1,0:T(8,128)} custom-call(bf16[128,4096]{1,0:T(8,128)(2,1)} %cot.1, bf16[128,4096]{1,0:T(8,128)(2,1)} %bitcast.19, bf16[128,4096]{1,0:T(8,128)(2,1)} %bitcast.20, bf16[128,4096]{1,0:T(8,128)(2,1)} %bitcast.21, bf16[128,256]{1,0:T(8,128)(2,1)} %bitcast.22), custom_call_target="tpu_custom_call" | custom-call | tf_op jit(solution)/shard_map/pallas_call | solution.py:416
  90.9 0.0 copy-done.1
  90.9 1.2 %rsqrt_multiply_fusion = f32[1,64]{1,0:T(1,128)} fusion(f32[1,64]{1,0:T(1,128)S(1)} %copy-done.1, f32[8,128]{1,0:T(8,128)} %shard_map.86), kind=kLoop, calls=%fused_computation.5 | loop fusion | flops 192 | bytes 768 | tf_op jit(solution)/shard_map/div | solution.py:403
  92.1 0.0 copy-done
  92.1 1.3 %fusion.2 = f32[1,128,4]{1,2,0:T(4,128)} fusion(f32[1,128,4]{1,2,0:T(4,128)S(1)} %copy-done, f32[8,128]{1,0:T(8,128)} %shard_map.86), kind=kLoop, calls=%fused_computation.3 | loop fusion | flops 1536 | bytes 6144 | tf_op jit(solution)/shard_map/broadcast_in_dim | solution.py:461
Async XLA Ops:
  0.6 90.3 %copy-start.1 = (f32[1,64]{1,0:T(1,128)S(1)}, f32[1,64]{1,0:T(1,128)}, u32[]{:S(2)}) copy-start(f32[1,64]{1,0:T(1,128)} %param.12) | copy-start | bytes 772
  0.6 91.5 %copy-start = (f32[1,128,4]{1,2,0:T(4,128)S(1)}, f32[1,128,4]{1,2,0:T(4,128)}, u32[]{:S(2)}) copy-start(f32[1,128,4]{1,2,0:T(4,128)} %param.13) | copy-start | bytes 6148
